TPU v7x, 32 devices: a whole 2x2x4 slice. The times are simulated.
32 devices in a mesh: nodes: 8 (over z, y), mp: 4 (over x, core).
Axes of the slice: x: 2, y: 2, z: 4, core: 2. Of those that a mesh axis runs over, the one named last changes fastest.
Arguments:
- query: bfloat16 [2048, 512], P('nodes', 'mp'), may hold values from -240 to 240
- key: bfloat16 [2048, 512], P('nodes', 'mp'), may hold values from -7 to 7
- value: bfloat16 [2048, 512], P('nodes', 'mp'), may hold values from -12 to 12
- out_weight: bfloat16 [512, 512], P('mp'), may hold values from -0.25 to 0.25
- cotangent: bfloat16 [2048, 512], P('nodes', 'mp'), may hold values from -6 to 6
- virtual_key: bfloat16 [64, 512], P('nodes', 'mp'), may hold values from -6 to 6
- virtual_value: bfloat16 [64, 512], P('nodes', 'mp'), may hold values from -12 to 12
- halo_rows: int32 [8, 2, 128], P('nodes'), may hold values from 0 to 255
- halo_live: int32 [8, 2], P('nodes'), may hold values from 64 to 128, as said below
- expand_rows: int32 [8, 8, 2], P('nodes'), may hold values from 0 to 255
- local_mask: int32 [16, 4], P('nodes'), may hold values from 0 to 1, as said below
- expand_mask: int32 [16, 8], P('nodes'), may hold values 0 or 1
Outputs:
- output: bfloat16 [2048, 512], P('nodes', 'mp')
- grad_query: float32 [2048, 512], P('nodes', 'mp')
- grad_key: float32 [2048, 512], P('nodes', 'mp')
- grad_value: float32 [2048, 512], P('nodes', 'mp')
- grad_virtual_key: float32 [64, 512], P('nodes', 'mp')
- grad_virtual_value: float32 [64, 512], P('nodes', 'mp')
Inputs may be any that keep to these rules, and one draw needn't show every extreme that they name: halo_rows[p, 0, :] index nodes of partition p (0 to 255) sent to partition p + 1, halo_rows[p, 1, :] those sent to partition p - 1; repeats possible. Only the leading halo_live slots of what a partition receives from a neighbour are edges; the value 128 occurs in every draw. expand_rows[r, p, :] index nodes of partition r. Every query tile attends its own tile and both received boundary tiles: local_mask[t, t mod 2], local_mask[t, 2] and local_mask[t, 3] are 1.
All inputs are finite; a program needn't handle non-finite values. No bound on the sum of `expand_mask` on one device may be relied on, other than what follows from the above.
Results may differ from a plain program's by a relative error of at most 0.034.
Values may be sent and summed in bfloat16 or wider, within the bound.
A program may use at most 64 MiB of HBM per device.

v0:
```python
import jax
import jax.numpy as jnp
from jax import lax
from jax.sharding import PartitionSpec as P

HEADS = 8


def extended(array, sides, width):
    for axis, dim in sides:
        devices, length = (lax.axis_size(axis), array.shape[dim])
        up = [(i, (i + 1) % devices) for i in range(devices)]
        down = [(j, i) for i, j in up]
        last = lax.slice_in_dim(array, length - width, length, axis=dim)
        leading = lax.slice_in_dim(array, 0, width, axis=dim)
        before = lax.ppermute(last, axis, up)
        after = lax.ppermute(leading, axis, down)
        array = jnp.concatenate([before, array, after], axis=dim)
    return array


def edge_mask(local_block, expand_block, live, tile_rows, halo_cap, exp_slot, virtual_count):
    tile_count = local_block.shape[0]
    own_tiles = jnp.repeat(
        jnp.repeat(local_block[:, :tile_count] > 0, tile_rows, axis=0), tile_rows, axis=1
    )
    slot_index = jnp.arange(halo_cap)
    left_ok = (local_block[:, tile_count] > 0)[:, None] & (slot_index < live[0])[None, :]
    right_ok = (local_block[:, tile_count + 1] > 0)[:, None] & (slot_index < live[1])[None, :]
    expand_ok = jnp.repeat(expand_block > 0, exp_slot, axis=1)
    remote_tiles = jnp.repeat(
        jnp.concatenate([left_ok, right_ok, expand_ok], axis=1), tile_rows, axis=0
    )
    virtual_ok = jnp.ones((tile_count * tile_rows, virtual_count), dtype=jnp.bool_)
    return jnp.concatenate([own_tiles, remote_tiles, virtual_ok], axis=1)


def body(
    query,
    key,
    value,
    out_weight,
    cotangent,
    virtual_key,
    virtual_value,
    halo_rows,
    halo_live,
    expand_rows,
    local_mask,
    expand_mask,
):
    node_rows, width = query.shape
    heads_dev = HEADS // lax.axis_size("mp")
    head_dim = width // heads_dev
    score_scale = head_dim ** (-0.5)
    tile_count = local_mask.shape[0]
    tile_rows = node_rows // tile_count
    halo_cap = halo_rows.shape[2]
    peer_count = expand_rows.shape[1]
    exp_slot = expand_rows.shape[2]
    to_right = halo_rows[0, 0]
    to_left = halo_rows[0, 1]
    expand_flat = expand_rows[0].reshape(-1)
    key_value = jnp.concatenate([key, value], axis=1)
    outgoing_rows = jnp.concatenate([key_value[to_left], key_value[to_right]], axis=0)
    padded = extended(outgoing_rows, (("nodes", 0),), halo_cap)
    from_left = padded[:halo_cap]
    from_right = padded[3 * halo_cap :]
    expand_sent = key_value[expand_flat].reshape(peer_count, exp_slot, 2 * width)
    arrived = lax.all_to_all(expand_sent, "nodes", split_axis=0, concat_axis=0, tiled=True).reshape(
        peer_count * exp_slot, 2 * width
    )
    all_virtual_key, all_virtual_value = (
        lax.all_gather(virtual_key, "nodes", axis=0, tiled=True),
        lax.all_gather(virtual_value, "nodes", axis=0, tiled=True),
    )
    virtual_count = all_virtual_key.shape[0]
    all_keys = jnp.concatenate(
        [key, from_left[:, :width], from_right[:, :width], arrived[:, :width], all_virtual_key],
        axis=0,
    )
    all_values = jnp.concatenate(
        [value, from_left[:, width:], from_right[:, width:], arrived[:, width:], all_virtual_value],
        axis=0,
    )
    allowed = edge_mask(
        local_mask, expand_mask, halo_live[0], tile_rows, halo_cap, exp_slot, virtual_count
    )
    d_attn = jnp.einsum(
        "nc,wc->nw",
        lax.all_gather(cotangent, "mp", axis=1, tiled=True),
        out_weight,
        preferred_element_type=jnp.float32,
    ).astype(jnp.bfloat16)
    attn_parts = []
    grad_query_parts = []
    grad_key_parts = []
    grad_value_parts = []
    for head_number in range(heads_dev):
        low = head_number * head_dim
        high = low + head_dim
        query_head = query[:, low:high]
        key_head = all_keys[:, low:high]
        value_head = all_values[:, low:high]
        grad_head = d_attn[:, low:high]
        scores = (
            jnp.einsum("qd,kd->qk", query_head, key_head, preferred_element_type=jnp.float32)
            * score_scale
        )
        scores = jnp.where(allowed, scores, -1e30)
        row_max = jnp.max(scores, axis=1, keepdims=True)
        weights = jnp.exp(scores - row_max)
        probs = weights / jnp.sum(weights, axis=1, keepdims=True)
        probs_b = probs.astype(jnp.bfloat16)
        attn_head = jnp.dot(probs_b, value_head, preferred_element_type=jnp.float32).astype(
            jnp.bfloat16
        )
        d_prob = jnp.einsum("qd,kd->qk", grad_head, value_head, preferred_element_type=jnp.float32)
        row_delta = jnp.sum(
            grad_head.astype(jnp.float32) * attn_head.astype(jnp.float32), axis=1, keepdims=True
        )
        d_score = (probs * (d_prob - row_delta) * score_scale).astype(jnp.bfloat16)
        attn_parts.append(attn_head)
        grad_query_parts.append(jnp.dot(d_score, key_head, preferred_element_type=jnp.float32))
        grad_key_parts.append(
            jnp.einsum("qk,qd->kd", d_score, query_head, preferred_element_type=jnp.float32)
        )
        grad_value_parts.append(
            jnp.einsum("qk,qd->kd", probs_b, grad_head, preferred_element_type=jnp.float32)
        )
    attn = jnp.concatenate(attn_parts, axis=1)
    grad_query = jnp.concatenate(grad_query_parts, axis=1)
    grad_keys = jnp.concatenate(grad_key_parts, axis=1)
    grad_values = jnp.concatenate(grad_value_parts, axis=1)
    projected = jnp.dot(attn, out_weight, preferred_element_type=jnp.float32)
    output = lax.psum_scatter(projected, "mp", scatter_dimension=1, tiled=True).astype(jnp.bfloat16)
    left_end = node_rows + halo_cap
    right_end = left_end + halo_cap
    expand_end = right_end + peer_count * exp_slot
    grad_pairs = jnp.concatenate([grad_keys, grad_values], axis=1)
    halo_back = grad_pairs[node_rows:right_end]
    returned = extended(halo_back, (("nodes", 0),), halo_cap)
    for_left_sent = returned[:halo_cap]
    for_right_sent = returned[3 * halo_cap :]
    expand_back = grad_pairs[right_end:expand_end].reshape(peer_count, exp_slot, 2 * width)
    came_home = lax.all_to_all(
        expand_back, "nodes", split_axis=0, concat_axis=0, tiled=True
    ).reshape(peer_count * exp_slot, 2 * width)
    own_grads = grad_pairs[:node_rows]
    own_grads = own_grads.at[to_left].add(for_left_sent)
    own_grads = own_grads.at[to_right].add(for_right_sent)
    own_grads = own_grads.at[expand_flat].add(came_home)
    grad_key = own_grads[:, :width]
    grad_value = own_grads[:, width:]
    virtual_key_term = grad_keys[expand_end:]
    virtual_value_term = grad_values[expand_end:]
    grad_virtual_key, grad_virtual_value = (
        lax.psum_scatter(virtual_key_term, "nodes", scatter_dimension=0, tiled=True),
        lax.psum_scatter(virtual_value_term, "nodes", scatter_dimension=0, tiled=True),
    )
    return (output, grad_query, grad_key, grad_value, grad_virtual_key, grad_virtual_value)


def solution(mesh):
    return jax.shard_map(
        body,
        mesh=mesh,
        in_specs=(
            P("nodes", "mp"),
            P("nodes", "mp"),
            P("nodes", "mp"),
            P("mp", None),
            P("nodes", "mp"),
            P("nodes", "mp"),
            P("nodes", "mp"),
            P("nodes", None, None),
            P("nodes", None),
            P("nodes", None, None),
            P("nodes", None),
            P("nodes", None),
        ),
        out_specs=(
            P("nodes", "mp"),
            P("nodes", "mp"),
            P("nodes", "mp"),
            P("nodes", "mp"),
            P("nodes", "mp"),
            P("nodes", "mp"),
        ),
        check_vma=False,
    )
```

profile of v0, /device:TPU:0, one launch (start us, length us, event | category | flops | bytes accessed | tf_op | source)
XLA Modules:
  0.0 192.0 jit_solution(5253378758399897791)
XLA Ops:
  8.0 0.8 copy.38
  8.9 0.9 constant_dynamic-update-slice_fusion.1
  11.0 7.4 %all-to-all-start = ((bf16[8,2,256]{2,1,0:T(2,128)(2,1)}), bf16[8,2,256]{2,1,0:T(2,128)(2,1)S(1)}, u32[]{:S(2)}, u32[]{:S(2)}) async-start(bf16[8,2,256]{2,1,0:T(2,128)(2,1)} %reshape.142), calls=%async_computation | async-start | bytes 16384 | tf_op jit(solution)/shard_map/all_to_all | solution.py:70
  18.5 0.8 gather_fusion
  19.3 2.1 %collective-permute-start = (bf16[128,256]{1,0:T(8,128)(2,1)S(1)}, bf16[128,256]{1,0:T(8,128)(2,1)S(1)}, u32[]{:S(2)}, u32[]{:S(2)}) collective-permute-start(bf16[128,256]{1,0:T(8,128)(2,1)S(1)} %gather_fusion), channel_id=1, source_target_pairs={{0,4},{4,8},{8,12},{12,16},{16,20},{20,24},{24,28},{28,0},{1,5},{5... | collective-permute-start | bytes 196616 | tf_op jit(solution)/shard_map/ppermute | solution.py:16
  21.4 0.8 gather_fusion.1
  22.3 2.8 %collective-permute-start.1 = (bf16[128,256]{1,0:T(8,128)(2,1)S(1)}, bf16[128,256]{1,0:T(8,128)(2,1)S(1)}, u32[]{:S(2)}, u32[]{:S(2)}) collective-permute-start(bf16[128,256]{1,0:T(8,128)(2,1)S(1)} %gather_fusion.1), channel_id=1, source_target_pairs={{4,0},{8,4},{12,8},{16,12},{20,16},{24,20},{28,24},{0,28},{5,1},{9... | collective-permute-start | bytes 196616 | tf_op jit(solution)/shard_map/ppermute | solution.py:17
  28.6 5.8 %all_gather.11 = bf16[256,512]{1,0:T(8,128)(2,1)S(1)} all-gather(bf16[256,128]{1,0:T(8,128)(2,1)S(1)} %copy-done.3), channel_id=1, replica_groups=mesh['nodes'=8,'mp'=4] {'mp'}, dimensions={1}, use_global_device_ids=true | all-gather | bytes 327680 | tf_op jit(solution)/shard_map/all_gather | solution.py:91
  37.5 26.1 %all_gather.9 = bf16[64,128]{1,0:T(8,128)(2,1)S(1)} all-gather(bf16[8,128]{1,0:T(8,128)(2,1)S(1)} %copy-done.6), channel_id=1, replica_groups=mesh['nodes'=8,'mp'=4] {'nodes'}, dimensions={0}, use_global_device_ids=true | all-gather | bytes 18432 | tf_op jit(solution)/shard_map/all_gather | solution.py:74
  63.7 26.0 %all_gather.10 = bf16[64,128]{1,0:T(8,128)(2,1)S(1)} all-gather(bf16[8,128]{1,0:T(8,128)(2,1)S(1)} %copy-done.7), channel_id=1, replica_groups=mesh['nodes'=8,'mp'=4] {'nodes'}, dimensions={0}, use_global_device_ids=true | all-gather | bytes 18432 | tf_op jit(solution)/shard_map/all_gather | solution.py:75
  89.8 0.8 copy-done.1
  93.8 0.7 pad_maximum_fusion.6
  94.6 0.7 pad_maximum_fusion.5
  96.0 3.3 %all-to-all-start.1 = ((f32[8,2,256]{2,1,0:T(2,128)}), f32[8,2,256]{2,1,0:T(2,128)S(1)}, u32[]{:S(2)}, u32[]{:S(2)}) async-start(f32[8,2,256]{2,1,0:T(2,128)} %reshape.144), calls=%async_computation.2 | async-start | bytes 32768 | tf_op jit(solution)/shard_map/all_to_all | solution.py:146
  99.4 1.0 fusion.26
  101.7 0.8 copy.43
  102.6 4.7 %collective-permute-start.3 = (f32[128,256]{0,1:T(8,128)S(1)}, f32[128,256]{0,1:T(8,128)S(1)}, u32[]{:S(2)}, u32[]{:S(2)}) collective-permute-start(f32[128,256]{0,1:T(8,128)S(1)} %get-tuple-element.30), channel_id=1, source_target_pairs={{4,0},{8,4},{12,8},{16,12},{20,16},{24,20},{28,24},{0,28},{5,1},{9... | collective-permute-start | bytes 393224 | tf_op jit(solution)/shard_map/ppermute | solution.py:17
  107.3 68.6 %all-reduce.5.cloned.1.call-done = (f32[64,128]{0,1:T(8,128)}, f32[64,128]{0,1:T(8,128)}) async-done(((f32[64,128]{0,1:T(8,128)}, f32[64,128]{0,1:T(8,128)}), (f32[64,128]{0,1:T(8,128)}, f32[64,128]{0,1:T(8,128)})) %all-reduce.5.cloned.1.call-update) | async-done | bytes 65552
  175.9 0.9 constant_dynamic-slice_fusion.1
  178.5 1.4 scatter_fusion
  180.1 1.4 scatter_fusion.1
  181.5 0.8 scatter_fusion.2
  182.3 0.7 fusion.46
  183.0 1.5 convert_element_type.40
  (100 shorter events, 14.5 us)
Async XLA Ops:
  8.0 26.4 %copy-start = (bf16[128,512]{1,0:T(8,128)(2,1)S(1)}, bf16[128,512]{1,0:T(8,128)(2,1)}, u32[]{:S(2)}) copy-start(bf16[128,512]{1,0:T(8,128)(2,1)} %param.15) | copy-start | bytes 393220
  8.9 0.9 copy-start.2
  11.0 7.4 %copy-start.9 = (s32[1,2,128]{2,1,0:T(2,128)S(1)}, s32[1,2,128]{2,1,0:T(2,128)}, u32[]{:S(2)}) copy-start(s32[1,2,128]{2,1,0:T(2,128)} %param.19) | copy-start | bytes 3076
  11.0 78.6 %all-to-all-start = ((bf16[8,2,256]{2,1,0:T(2,128)(2,1)}), bf16[8,2,256]{2,1,0:T(2,128)(2,1)S(1)}, u32[]{:S(2)}, u32[]{:S(2)}) async-start(bf16[8,2,256]{2,1,0:T(2,128)(2,1)} %reshape.142), calls=%async_computation | async-start | bytes 16384 | tf_op jit(solution)/shard_map/all_to_all | solution.py:70
  19.3 70.3 %collective-permute-start = (bf16[128,256]{1,0:T(8,128)(2,1)S(1)}, bf16[128,256]{1,0:T(8,128)(2,1)S(1)}, u32[]{:S(2)}, u32[]{:S(2)}) collective-permute-start(bf16[128,256]{1,0:T(8,128)(2,1)S(1)} %gather_fusion), channel_id=1, source_target_pairs={{0,4},{4,8},{8,12},{12,16},{16,20},{20,24},{24,28},{28,0},{1,5},{5... | collective-permute-start | bytes 196616 | tf_op jit(solution)/shard_map/ppermute | solution.py:16
  21.4 3.6 %copy-start.5 = (s32[2,4]{1,0:T(2,128)S(1)}, s32[2,4]{1,0:T(2,128)}, u32[]{:S(2)}) copy-start(s32[2,4]{1,0:T(2,128)} %param.22) | copy-start | bytes 100
  21.4 7.2 %copy-start.3 = (bf16[256,128]{1,0:T(8,128)(2,1)S(1)}, bf16[256,128]{1,0:T(8,128)(2,1)}, u32[]{:S(2)}) copy-start(bf16[256,128]{1,0:T(8,128)(2,1)} %param.16) | copy-start | bytes 196612
  22.3 67.4 %collective-permute-start.1 = (bf16[128,256]{1,0:T(8,128)(2,1)S(1)}, bf16[128,256]{1,0:T(8,128)(2,1)S(1)}, u32[]{:S(2)}, u32[]{:S(2)}) collective-permute-start(bf16[128,256]{1,0:T(8,128)(2,1)S(1)} %gather_fusion.1), channel_id=1, source_target_pairs={{4,0},{8,4},{12,8},{16,12},{20,16},{24,20},{28,24},{0,28},{5,1},{9... | collective-permute-start | bytes 196616 | tf_op jit(solution)/shard_map/ppermute | solution.py:17
  25.1 0.7 copy-start.10
  25.9 0.7 copy-start.8
  35.0 0.7 copy-start.11
  36.9 0.7 copy-start.6
  37.5 26.1 %copy-start.7 = (bf16[8,128]{1,0:T(8,128)(2,1)S(1)}, bf16[8,128]{1,0:T(8,128)(2,1)}, u32[]{:S(2)}) copy-start(bf16[8,128]{1,0:T(8,128)(2,1)} %param.18) | copy-start | bytes 6148
  89.7 0.8 copy-start.1
  96.0 11.2 %all-to-all-start.1 = ((f32[8,2,256]{2,1,0:T(2,128)}), f32[8,2,256]{2,1,0:T(2,128)S(1)}, u32[]{:S(2)}, u32[]{:S(2)}) async-start(f32[8,2,256]{2,1,0:T(2,128)} %reshape.144), calls=%async_computation.2 | async-start | bytes 32768 | tf_op jit(solution)/shard_map/all_to_all | solution.py:146
  99.4 76.5 %all-reduce.5.cloned.1.call-start = ((), (), s32[]{:S(2)}) async-start(), calls=%async_computation.4 | async-start | bytes 262144
  100.5 82.5 %reduce-scatter.4.cloned.1.call-start = ((), (), s32[]{:S(2)}) async-start(), calls=%async_computation.3 | async-start | bytes 655360 | tf_op jit(solution)/shard_map/reduce_scatter | solution.py:136
  102.6 77.4 %collective-permute-start.3 = (f32[128,256]{0,1:T(8,128)S(1)}, f32[128,256]{0,1:T(8,128)S(1)}, u32[]{:S(2)}, u32[]{:S(2)}) collective-permute-start(f32[128,256]{0,1:T(8,128)S(1)} %get-tuple-element.30), channel_id=1, source_target_pairs={{4,0},{8,4},{12,8},{16,12},{20,16},{24,20},{28,24},{0,28},{5,1},{9... | collective-permute-start | bytes 393224 | tf_op jit(solution)/shard_map/ppermute | solution.py:17
  107.2 71.2 %collective-permute-start.2 = (f32[128,256]{0,1:T(8,128)S(1)}, f32[128,256]{0,1:T(8,128)S(1)}, u32[]{:S(2)}, u32[]{:S(2)}) collective-permute-start(f32[128,256]{0,1:T(8,128)S(1)} %get-tuple-element.31), channel_id=1, source_target_pairs={{0,4},{4,8},{8,12},{12,16},{16,20},{20,24},{24,28},{28,0},{1,5},{5... | collective-permute-start | bytes 393224 | tf_op jit(solution)/shard_map/ppermute | solution.py:16
  176.8 0.8 copy-start.4
Sparse Core Ops, SparseCore 0:
  104.7 71.2 all-reduce.4
Sparse Core Ops, SparseCore 1:
  103.5 22.9 reduce-scatter.3
where the time goes:
time: 193 us; the launch traced here: 192 us
  waiting for transfers between devices  69.2 us (36%)
  blocking collectives  57.9 us (30%)
  starting transfers between devices  20.4 us (11%)
  between operations  16.5 us (9%)
  local copies, waits for them, and re-layouts  14.7 us (8%)
  other arithmetic  8.82 us (5%)
  matrix products  4.52 us (2%)
    unnamed x3, waiting for transfers between devices  69.2 us
    all_gather x1, blocking collectives, body(): lax.all_gather(virtual_key, 'nodes', axis=0, tiled=True)  26.1 us
    all_gather x1, blocking collectives, body(): lax.all_gather(virtual_value, 'nodes', axis=0, tiled=True)  26 us
    unnamed x38, local copies, waits for them, and re-layouts  8.75 us
    ppermute x2, starting transfers between devices, extended(): after = lax.ppermute(leading, axis, down)  7.45 us
    all_to_all x1, starting transfers between devices, body(): lax.all_to_all(expand_sent, 'nodes', split_axis=0, concat_axis=0, tiled=T...  7.41 us
    all_gather x1, blocking collectives, body(): lax.all_gather(cotangent, 'mp', axis=1, tiled=True)  5.81 us
  transfers between devices with their start and end apart: 8, of which 1 were waited for; matrix products, arithmetic and copies ran while one was open for 8% of the time, Pallas kernels for 0%

commit v1 on v0

--- a/solution.py
+++ b/solution.py
@@ -4,6 +4,18 @@
 from jax.sharding import PartitionSpec as P
 
 HEADS = 8
+
+
+def collect(array, axis, dim):
+    ways, here = (lax.axis_size(axis), lax.axis_index(axis))
+    grown, reach = (array, 1)
+    while reach < ways:
+        theirs = lax.ppermute(grown, axis, [(d, d ^ reach) for d in range(ways)])
+        mine_first = jnp.concatenate([grown, theirs], axis=dim)
+        theirs_first = jnp.concatenate([theirs, grown], axis=dim)
+        grown = jnp.where(here & reach == 0, mine_first, theirs_first)
+        reach = 2 * reach
+    return grown
 
 
 def extended(array, sides, width):
@@ -72,7 +84,7 @@
     )
     all_virtual_key, all_virtual_value = (
         lax.all_gather(virtual_key, "nodes", axis=0, tiled=True),
-        lax.all_gather(virtual_value, "nodes", axis=0, tiled=True),
+        collect(virtual_value, "nodes", 0),
     )
     virtual_count = all_virtual_key.shape[0]
     all_keys = jnp.concatenate(

time: 193 us -> 170 us (0.88)
  blocking collectives: 57.9 us -> 31.8 us
  waiting for transfers between devices: 69.2 us -> 71.9 us
    all_gather x1 -> x0, blocking collectives: 26 us -> none  [body(): lax.all_gather(virtual_value, 'nodes', axis=0, tiled=True)]
    ppermute x0 -> x3, starting transfers between devices: none -> 3.29 us  [collect(): theirs = lax.ppermute(grown, axis, [(d, d ^ reach) for d in range(ways)])]
    ppermute x0 -> x3, waiting for transfers between devices: none -> 2.69 us  [collect(): theirs = lax.ppermute(grown, axis, [(d, d ^ reach) for d in range(ways)])]
    all_to_all x1, starting transfers between devices: 7.41 us -> 5.01 us  [body(): lax.all_to_all(expand_sent, 'nodes', split_axis=0, concat_axis=0, tiled=T...]
  transfers between devices with their start and end apart: 8 -> 11, of which waited for: 1 -> 2; matrix products, arithmetic and copies ran while one was open for 8% -> 11% of each run, Pallas kernels for 0% -> 0%
where the time goes in v1:
time: 170 us; the launch traced here: 169 us
  waiting for transfers between devices  71.9 us (42%)
  blocking collectives  31.8 us (19%)
  starting transfers between devices  21.2 us (12%)
  between operations  16.5 us (10%)
  local copies, waits for them, and re-layouts  14.6 us (9%)
  other arithmetic  8.84 us (5%)
  matrix products  4.52 us (3%)
    unnamed x3, waiting for transfers between devices  69.2 us
    all_gather x1, blocking collectives, body(): lax.all_gather(virtual_key, 'nodes', axis=0, tiled=True)  26 us
    unnamed x38, local copies, waits for them, and re-layouts  8.71 us
    ppermute x2, starting transfers between devices, extended(): after = lax.ppermute(leading, axis, down)  7.45 us
    all_gather x1, blocking collectives, body(): lax.all_gather(cotangent, 'mp', axis=1, tiled=True)  5.81 us
    all_to_all x1, starting transfers between devices, body(): lax.all_to_all(expand_sent, 'nodes', split_axis=0, concat_axis=0, tiled=T...  5.01 us
  transfers between devices with their start and end apart: 11, of which 2 were waited for; matrix products, arithmetic and copies ran while one was open for 11% of the time, Pallas kernels for 0%

profile of v1, /device:TPU:0, one launch (start us, length us, event | category | flops | bytes accessed | tf_op | source)
XLA Modules:
  0.0 169.4 jit_solution(16647566277897796874)
XLA Ops:
  8.0 3.0 %collective-permute-start.2 = (bf16[8,128]{1,0:T(8,128)(2,1)}, bf16[8,128]{1,0:T(8,128)(2,1)S(1)}, u32[]{:S(2)}, u32[]{:S(2)}) collective-permute-start(bf16[8,128]{1,0:T(8,128)(2,1)} %param.18), channel_id=1, source_target_pairs={{0,4},{4,0},{8,12},{12,8},{16,20},{20,16},{24,28},{28,24},{1,5},{5... | collective-permute-start | bytes 6152 | tf_op jit(solution)/shard_map/ppermute | solution.py:13
  11.0 0.8 copy.38
  11.9 0.9 constant_dynamic-update-slice_fusion.1
  14.0 5.0 %all-to-all-start = ((bf16[8,2,256]{2,1,0:T(2,128)(2,1)}), bf16[8,2,256]{2,1,0:T(2,128)(2,1)S(1)}, u32[]{:S(2)}, u32[]{:S(2)}) async-start(bf16[8,2,256]{2,1,0:T(2,128)(2,1)} %reshape.142), calls=%async_computation | async-start | bytes 16384 | tf_op jit(solution)/shard_map/all_to_all | solution.py:82
  19.1 0.8 gather_fusion
  19.9 2.1 %collective-permute-start = (bf16[128,256]{1,0:T(8,128)(2,1)S(1)}, bf16[128,256]{1,0:T(8,128)(2,1)S(1)}, u32[]{:S(2)}, u32[]{:S(2)}) collective-permute-start(bf16[128,256]{1,0:T(8,128)(2,1)S(1)} %gather_fusion), channel_id=1, source_target_pairs={{0,4},{4,8},{8,12},{12,16},{16,20},{20,24},{24,28},{28,0},{1,5},{5... | collective-permute-start | bytes 196616 | tf_op jit(solution)/shard_map/ppermute | solution.py:28
  22.0 0.8 gather_fusion.1
  22.9 2.8 %collective-permute-start.1 = (bf16[128,256]{1,0:T(8,128)(2,1)S(1)}, bf16[128,256]{1,0:T(8,128)(2,1)S(1)}, u32[]{:S(2)}, u32[]{:S(2)}) collective-permute-start(bf16[128,256]{1,0:T(8,128)(2,1)S(1)} %gather_fusion.1), channel_id=1, source_target_pairs={{4,0},{8,4},{12,8},{16,12},{20,16},{24,20},{28,24},{0,28},{5,1},{9... | collective-permute-start | bytes 196616 | tf_op jit(solution)/shard_map/ppermute | solution.py:29
  29.2 5.8 %all_gather.7 = bf16[256,512]{1,0:T(8,128)(2,1)S(1)} all-gather(bf16[256,128]{1,0:T(8,128)(2,1)S(1)} %copy-done.3), channel_id=1, replica_groups=mesh['nodes'=8,'mp'=4] {'mp'}, dimensions={1}, use_global_device_ids=true | all-gather | bytes 327680 | tf_op jit(solution)/shard_map/all_gather | solution.py:103
  38.3 26.0 %all_gather.6 = bf16[64,128]{1,0:T(8,128)(2,1)S(1)} all-gather(bf16[8,128]{1,0:T(8,128)(2,1)S(1)} %copy-done.7), channel_id=1, replica_groups=mesh['nodes'=8,'mp'=4] {'nodes'}, dimensions={0}, use_global_device_ids=true | all-gather | bytes 18432 | tf_op jit(solution)/shard_map/all_gather | solution.py:86
  64.6 0.8 copy-done.1
  66.3 2.7 %collective-permute-done.4 = bf16[32,128]{1,0:T(8,128)(2,1)S(1)} collective-permute-done((bf16[32,128]{1,0:T(8,128)(2,1)S(1)}, bf16[32,128]{1,0:T(8,128)(2,1)S(1)}, u32[]{:S(2)}, u32[]{:S(2)}) %collective-permute-start.4) | collective-permute-done | bytes 8224 | tf_op jit(solution)/shard_map/ppermute | solution.py:13
  71.3 0.7 pad_maximum_fusion.6
  73.5 3.3 %all-to-all-start.1 = ((f32[8,2,256]{2,1,0:T(2,128)}), f32[8,2,256]{2,1,0:T(2,128)S(1)}, u32[]{:S(2)}, u32[]{:S(2)}) async-start(f32[8,2,256]{2,1,0:T(2,128)} %reshape.144), calls=%async_computation.2 | async-start | bytes 32768 | tf_op jit(solution)/shard_map/all_to_all | solution.py:158
  76.9 1.0 fusion.26
  79.1 0.8 copy.43
  80.0 4.7 %collective-permute-start.6 = (f32[128,256]{0,1:T(8,128)S(1)}, f32[128,256]{0,1:T(8,128)S(1)}, u32[]{:S(2)}, u32[]{:S(2)}) collective-permute-start(f32[128,256]{0,1:T(8,128)S(1)} %get-tuple-element.30), channel_id=1, source_target_pairs={{4,0},{8,4},{12,8},{16,12},{20,16},{24,20},{28,24},{0,28},{5,1},{9... | collective-permute-start | bytes 393224 | tf_op jit(solution)/shard_map/ppermute | solution.py:29
  84.7 68.7 %all-reduce.5.cloned.1.call-done = (f32[64,128]{0,1:T(8,128)}, f32[64,128]{0,1:T(8,128)}) async-done(((f32[64,128]{0,1:T(8,128)}, f32[64,128]{0,1:T(8,128)}), (f32[64,128]{0,1:T(8,128)}, f32[64,128]{0,1:T(8,128)})) %all-reduce.5.cloned.1.call-update) | async-done | bytes 65552
  153.4 0.9 constant_dynamic-slice_fusion.1
  156.0 1.4 scatter_fusion
  157.5 1.4 scatter_fusion.1
  158.9 0.8 scatter_fusion.2
  159.7 0.7 fusion.46
  160.5 1.5 convert_element_type.40
  (107 shorter events, 15.4 us)
Async XLA Ops:
  8.0 27.0 %copy-start = (bf16[128,512]{1,0:T(8,128)(2,1)S(1)}, bf16[128,512]{1,0:T(8,128)(2,1)}, u32[]{:S(2)}) copy-start(bf16[128,512]{1,0:T(8,128)(2,1)} %param.15) | copy-start | bytes 393220
  8.0 29.5 %collective-permute-start.2 = (bf16[8,128]{1,0:T(8,128)(2,1)}, bf16[8,128]{1,0:T(8,128)(2,1)S(1)}, u32[]{:S(2)}, u32[]{:S(2)}) collective-permute-start(bf16[8,128]{1,0:T(8,128)(2,1)} %param.18), channel_id=1, source_target_pairs={{0,4},{4,0},{8,12},{12,8},{16,20},{20,16},{24,28},{28,24},{1,5},{5... | collective-permute-start | bytes 6152 | tf_op jit(solution)/shard_map/ppermute | solution.py:13
  11.9 0.9 copy-start.2
  14.0 5.0 %copy-start.9 = (s32[1,2,128]{2,1,0:T(2,128)S(1)}, s32[1,2,128]{2,1,0:T(2,128)}, u32[]{:S(2)}) copy-start(s32[1,2,128]{2,1,0:T(2,128)} %param.19) | copy-start | bytes 3076
  14.0 50.4 %all-to-all-start = ((bf16[8,2,256]{2,1,0:T(2,128)(2,1)}), bf16[8,2,256]{2,1,0:T(2,128)(2,1)S(1)}, u32[]{:S(2)}, u32[]{:S(2)}) async-start(bf16[8,2,256]{2,1,0:T(2,128)(2,1)} %reshape.142), calls=%async_computation | async-start | bytes 16384 | tf_op jit(solution)/shard_map/all_to_all | solution.py:82
  19.9 44.5 %collective-permute-start = (bf16[128,256]{1,0:T(8,128)(2,1)S(1)}, bf16[128,256]{1,0:T(8,128)(2,1)S(1)}, u32[]{:S(2)}, u32[]{:S(2)}) collective-permute-start(bf16[128,256]{1,0:T(8,128)(2,1)S(1)} %gather_fusion), channel_id=1, source_target_pairs={{0,4},{4,8},{8,12},{12,16},{16,20},{20,24},{24,28},{28,0},{1,5},{5... | collective-permute-start | bytes 196616 | tf_op jit(solution)/shard_map/ppermute | solution.py:28
  22.0 3.6 %copy-start.5 = (s32[2,4]{1,0:T(2,128)S(1)}, s32[2,4]{1,0:T(2,128)}, u32[]{:S(2)}) copy-start(s32[2,4]{1,0:T(2,128)} %param.22) | copy-start | bytes 100
  22.0 7.2 %copy-start.3 = (bf16[256,128]{1,0:T(8,128)(2,1)S(1)}, bf16[256,128]{1,0:T(8,128)(2,1)}, u32[]{:S(2)}) copy-start(bf16[256,128]{1,0:T(8,128)(2,1)} %param.16) | copy-start | bytes 196612
  22.9 41.6 %collective-permute-start.1 = (bf16[128,256]{1,0:T(8,128)(2,1)S(1)}, bf16[128,256]{1,0:T(8,128)(2,1)S(1)}, u32[]{:S(2)}, u32[]{:S(2)}) collective-permute-start(bf16[128,256]{1,0:T(8,128)(2,1)S(1)} %gather_fusion.1), channel_id=1, source_target_pairs={{4,0},{8,4},{12,8},{16,12},{20,16},{24,20},{28,24},{0,28},{5,1},{9... | collective-permute-start | bytes 196616 | tf_op jit(solution)/shard_map/ppermute | solution.py:29
  25.7 0.7 copy-start.10
  26.5 0.7 copy-start.8
  35.6 0.7 copy-start.11
  37.5 0.7 copy-start.6
  37.6 0.8 copy-start.7
  38.1 26.2 %collective-permute-start.3 = (bf16[16,128]{1,0:T(8,128)(2,1)S(1)}, bf16[16,128]{1,0:T(8,128)(2,1)S(1)}, u32[]{:S(2)}, u32[]{:S(2)}) collective-permute-start(bf16[16,128]{1,0:T(8,128)(2,1)S(1)} %maximum_select_fusion.2), channel_id=1, source_target_pairs={{0,8},{4,12},{8,0},{12,4},{16,24},{20,28},{24,16},{28,20},{1,9},{5... | collective-permute-start | bytes 12296 | tf_op jit(solution)/shard_map/ppermute | solution.py:13
  64.3 4.6 %collective-permute-start.4 = (bf16[32,128]{1,0:T(8,128)(2,1)S(1)}, bf16[32,128]{1,0:T(8,128)(2,1)S(1)}, u32[]{:S(2)}, u32[]{:S(2)}) collective-permute-start(bf16[32,128]{1,0:T(8,128)(2,1)S(1)} %maximum_select_fusion.1), channel_id=1, source_target_pairs={{0,16},{4,20},{8,24},{12,28},{16,0},{20,4},{24,8},{28,12},{1,17},{... | collective-permute-start | bytes 24584 | tf_op jit(solution)/shard_map/ppermute | solution.py:13
  64.5 0.8 copy-start.1
  73.5 11.2 %all-to-all-start.1 = ((f32[8,2,256]{2,1,0:T(2,128)}), f32[8,2,256]{2,1,0:T(2,128)S(1)}, u32[]{:S(2)}, u32[]{:S(2)}) async-start(f32[8,2,256]{2,1,0:T(2,128)} %reshape.144), calls=%async_computation.2 | async-start | bytes 32768 | tf_op jit(solution)/shard_map/all_to_all | solution.py:158
  76.8 76.5 %all-reduce.5.cloned.1.call-start = ((), (), s32[]{:S(2)}) async-start(), calls=%async_computation.4 | async-start | bytes 262144
  77.9 82.5 %reduce-scatter.4.cloned.1.call-start = ((), (), s32[]{:S(2)}) async-start(), calls=%async_computation.3 | async-start | bytes 655360 | tf_op jit(solution)/shard_map/reduce_scatter | solution.py:148
  80.0 77.4 %collective-permute-start.6 = (f32[128,256]{0,1:T(8,128)S(1)}, f32[128,256]{0,1:T(8,128)S(1)}, u32[]{:S(2)}, u32[]{:S(2)}) collective-permute-start(f32[128,256]{0,1:T(8,128)S(1)} %get-tuple-element.30), channel_id=1, source_target_pairs={{4,0},{8,4},{12,8},{16,12},{20,16},{24,20},{28,24},{0,28},{5,1},{9... | collective-permute-start | bytes 393224 | tf_op jit(solution)/shard_map/ppermute | solution.py:29
  84.7 71.2 %collective-permute-start.5 = (f32[128,256]{0,1:T(8,128)S(1)}, f32[128,256]{0,1:T(8,128)S(1)}, u32[]{:S(2)}, u32[]{:S(2)}) collective-permute-start(f32[128,256]{0,1:T(8,128)S(1)} %get-tuple-element.31), channel_id=1, source_target_pairs={{0,4},{4,8},{8,12},{12,16},{16,20},{20,24},{24,28},{28,0},{1,5},{5... | collective-permute-start | bytes 393224 | tf_op jit(solution)/shard_map/ppermute | solution.py:28
  154.3 0.8 copy-start.4
Sparse Core Ops, SparseCore 0:
  82.1 71.2 all-reduce.4
Sparse Core Ops, SparseCore 1:
  80.9 22.9 reduce-scatter.3
